TPU v7x, 32 devices: a whole 2x2x4 slice. The times are simulated.
32 devices in a mesh: patch: 2 (over y), epoch: 4 (over z), tile: 4 (over x, core).
Axes of the slice: x: 2, y: 2, z: 4, core: 2. Of those that a mesh axis runs over, the one named last changes fastest.
Arguments:
- template: float32 [768, 512], P(('patch', 'epoch'), 'tile'), parts along dimension 0, may hold values from -14.2 to 14.2
- science: float32 [8, 384, 512], P(('patch', 'epoch'), None, 'tile'), parts along dimension 0, may hold values from -31 to 31
- row_profiles: float32 [12, 21], replicated, may hold values from -1.25 to 1.25
- col_profiles: float32 [12, 21], replicated, may hold values from -1.25 to 1.25
- coverage: int32 [8, 256], P(('patch', 'epoch'), 'tile'), parts along dimension 0, may hold values 0 or 1
- stamp_rows: int32 [512], P(('patch', 'tile')), parts along dimension 0, may hold values from 0 to 352
- stamp_cols: int32 [512], P(('patch', 'tile')), parts along dimension 0, may hold values from 0 to 96
Outputs:
- difference: float32 [8, 384, 512], P(('patch', 'epoch'), None, 'tile'), parts along dimension 0
There are 2 independent parts, one for each index of `patch`. A program takes and returns all parts, laid end to end along the dimension named above; an argument that names none is the same for every part. Nothing has to cross between parts.
All inputs are finite; a program needn't handle non-finite values. No bound on the sum of `coverage` on one device may be relied on, other than what follows from the above.
Results may differ from a plain program's by a relative error of at most 0.00011.
Values sent between devices are 32-bit elements; how exact they have to be, the bound alone decides.
A program may use at most 128 MiB of HBM per device.

v0:
```python
import functools

import jax
import jax.numpy as jnp
from jax import lax
from jax.experimental import pallas as pl
from jax.experimental.pallas import tpu as pltpu
from jax.sharding import PartitionSpec as P

S = 32
GROUP = 16
LANES = 128
ridge_weight = 1.0
F32 = jnp.float32
BF16 = jnp.bfloat16
NT = (((1,), (1,)), ((), ()))
NN = (((1,), (0,)), ((), ()))


def split(value):
    high = value.astype(BF16)
    return high, (value - high.astype(F32)).astype(BF16)


def dot3(left, right, dims):
    left_high, left_low = left
    right_high, right_low = right
    dot = functools.partial(lax.dot_general, dimension_numbers=dims, preferred_element_type=F32)
    return dot(left_high, right_high) + (dot(left_high, right_low) + dot(left_low, right_high))


def toeplitz(profile_row, rows, shift, width):
    base = pltpu.roll(jnp.broadcast_to(profile_row, (8, width)), 0, 1, stride=1, stride_axis=0)
    turns = [(shift + first) % width for first in range(0, rows, 8)]
    return jnp.concatenate([pltpu.roll(base, turn, 1) if turn else base for turn in turns], axis=0)


def iota(shape, axis):
    return lax.broadcasted_iota(jnp.int32, shape, axis)


def row_block(rows, extra, width):
    best = 8
    for size in range(8, width - extra + 1, 8):
        if rows % size == 0:
            best = size
    return best


def xi_row(cols, total):
    start = lax.axis_index("tile") * cols
    return 2.0 * (start + iota((1, cols), 1)).astype(F32) / total - 1.0


def convolve(strip, rowp_ref, colp_ref, images_ref, mixed_ref, taps):
    count, rows, cols = images_ref.shape
    width = 2 * LANES
    half = taps // 2
    block = row_block(rows, taps - 1, width)
    strip = split(strip)
    for b in range(count):
        band = split(toeplitz(colp_ref[b : b + 1, :], cols, -half, width))
        across = dot3(strip, band, NT)
        across = split(across)
        band = split(toeplitz(rowp_ref[b : b + 1, :], block, 0, width))
        for start in range(0, rows, block):
            piece = dot3(band, tuple(part[start : start + width] for part in across), NN)
            images_ref[b, start : start + block, :] = piece
            mixed_ref[pl.ds(start * GROUP + b, block, stride=GROUP), :] = piece


def gram(srow_ref, scol_ref, cov_ref, mixed_ref, rows, cols, total):
    stamps = srow_ref.shape[1]
    at = iota((stamps, cols), 1) - scol_ref[...]
    cols_in = jnp.where((at >= 0) & (at < S), cov_ref[...].astype(F32), 0.0).astype(BF16)
    xi = xi_row(cols, total)
    step = 16
    size = step * GROUP

    def body(chunk, acc):
        y = chunk * step + iota((size, 1), 0) // GROUP
        at_row = y - srow_ref[...]
        rows_in = jnp.where((at_row >= 0) & (at_row < S), 1.0, 0.0).astype(BF16)
        weight = lax.dot_general(rows_in, cols_in, NN, preferred_element_type=F32)
        base = mixed_ref[pl.ds(pl.multiple_of(chunk * size, size), size), :]
        eta = 2.0 * y.astype(F32) / rows - 1.0
        feats = (base, base * xi, base * eta)

        def lay(values):
            return jnp.concatenate(
                [
                    jnp.concatenate([v[k * GROUP : (k + 1) * GROUP] for k in range(step)], axis=1)
                    for v in values
                ],
                axis=0,
            )

        right = split(lay(feats))
        left = split(lay([f * weight for f in feats]))
        return acc + dot3(left, right, NT)

    return lax.fori_loop(0, rows // step, body, jnp.zeros((3 * GROUP, 3 * GROUP), F32))


def solve(normal, count):
    side = 3 * GROUP
    row, col = iota((side, LANES), 0), iota((side, LANES), 1)

    def used(k):
        return ((k % GROUP < count) & (k < side)) | (k == count)

    normal = jnp.concatenate([normal, jnp.zeros((side, LANES - side), F32)], axis=1)
    rhs = normal[:, count + 1 : count + 2]
    system = jnp.where(used(row) & used(col), normal, 0.0) + ridge_weight * jnp.where(row == col, 1.0, 0.0)
    system = jnp.where((col == side) & used(row), rhs, system)
    unknowns = [k for k in range(side) if (k % GROUP < count) or k == count]
    for p in unknowns:
        pivot_row = system[p : p + 1, :]
        factor = system[:, p : p + 1] / system[p : p + 1, p : p + 1]
        factor = jnp.where(row[:, :1] == p, 0.0, factor)
        system = system - factor * pivot_row
    diagonal = jnp.sum(jnp.where(row == col, system, 0.0), axis=1, keepdims=True)
    return system[:, side : side + 1] / diagonal


def apply(coefs, images_ref, science_ref, out_ref, total):
    count, rows, cols = images_ref.shape
    xi = xi_row(cols, total)
    eta = 2.0 * iota((rows, 1), 0).astype(F32) / rows - 1.0
    field = jnp.broadcast_to(coefs[count : count + 1, :], (rows, cols))
    for b in range(count):
        flat = coefs[b : b + 1] + coefs[GROUP + b : GROUP + b + 1] * xi
        field = field + images_ref[b] * (flat + coefs[2 * GROUP + b : 2 * GROUP + b + 1] * eta)
    out_ref[0] = science_ref[0] - field


def fill_rest(mixed_ref, science, count):
    rows = science.shape[0]
    mixed_ref[pl.ds(count, rows, stride=GROUP), :] = jnp.ones_like(science)
    mixed_ref[pl.ds(count + 1, rows, stride=GROUP), :] = science
    for spare in range(count + 2, GROUP):
        mixed_ref[pl.ds(spare, rows, stride=GROUP), :] = jnp.zeros_like(science)


def front(taps, total, strip_ref, side_ref, science_ref, rowp_ref, colp_ref, cov_ref, srow_ref, scol_ref,
          images_ref, gram_ref, mixed_ref):
    count, rows, cols = images_ref.shape
    fill_rest(mixed_ref, science_ref[0], count)
    strip = jnp.concatenate([strip_ref[...], side_ref[...]], axis=1)
    convolve(strip, rowp_ref, colp_ref, images_ref, mixed_ref, taps)
    gram_ref[...] = gram(srow_ref, scol_ref, cov_ref, mixed_ref, rows, cols, total)


def back(total, gram_ref, images_ref, science_ref, out_ref):
    coefs = solve(gram_ref[...], images_ref.shape[0])
    apply(coefs, images_ref, science_ref, out_ref, total)


def local(template, science, row_profiles, col_profiles, coverage, stamp_rows, stamp_cols):
    count, taps = row_profiles.shape
    half = taps // 2
    rows, cols = science.shape[1:]
    tiles = lax.axis_size("tile")
    total = cols * tiles
    width = 2 * LANES
    block = row_block(rows, taps - 1, width)
    high = rows - block + width
    column = lax.all_gather(template, "epoch", axis=0, tiled=True)
    right = lax.ppermute(column[:, :half], "tile", [(i + 1, i) for i in range(tiles - 1)])
    left = lax.ppermute(column[:, cols - half :], "tile", [(i, i + 1) for i in range(tiles - 1)])
    side = jnp.concatenate([right, jnp.zeros((rows, LANES - 2 * half), F32), left], axis=1)
    pads = ((half, high - rows - half), (0, 0))
    fit = ((0, 0), (0, width - taps))
    vmem = pl.BlockSpec(memory_space=pltpu.VMEM)
    images, normal = pl.pallas_call(
        functools.partial(front, taps, total),
        out_shape=(
            jax.ShapeDtypeStruct((count, rows, cols), F32),
            jax.ShapeDtypeStruct((3 * GROUP, 3 * GROUP), F32),
        ),
        in_specs=[vmem] * 8,
        out_specs=(vmem, vmem),
        scratch_shapes=[pltpu.VMEM((rows * GROUP, cols), F32)],
        compiler_params=pltpu.CompilerParams(vmem_limit_bytes=48 * 2**20),
    )(
        jnp.pad(column, pads),
        jnp.pad(side, pads),
        science,
        jnp.pad(row_profiles, fit),
        jnp.pad(col_profiles, fit),
        coverage.reshape(-1, 1),
        stamp_rows.reshape(1, -1),
        stamp_cols.reshape(-1, 1),
    )
    normal = lax.psum(normal, "tile")
    return pl.pallas_call(
        functools.partial(back, total),
        out_shape=jax.ShapeDtypeStruct(science.shape, F32),
        in_specs=[vmem] * 3,
        out_specs=vmem,
        compiler_params=pltpu.CompilerParams(vmem_limit_bytes=48 * 2**20),
    )(normal, images, science)


def solution(mesh):
    in_specs = (
        P(("patch", "epoch"), "tile"),
        P(("patch", "epoch"), None, "tile"),
        P(),
        P(),
        P(("patch", "epoch"), "tile"),
        P(("patch", "tile")),
        P(("patch", "tile")),
    )
    out_specs = P(("patch", "epoch"), None, "tile")
    return jax.shard_map(local, mesh=mesh, in_specs=in_specs, out_specs=out_specs, check_vma=False)
```

profile of v0, /device:TPU:0, one launch (start us, length us, event | category | flops | bytes accessed | tf_op | source)
XLA Modules:
  0.0 58.9 jit_solution(3464004953826426753)
XLA Ops:
  0.0 0.0 copy-start
  0.0 0.0 copy-start.1
  0.0 15.8 %all_gather.3 = f32[384,128]{1,0:T(8,128)S(1)} all-gather(f32[96,128]{1,0:T(8,128)} %param.7), channel_id=1, replica_groups=mesh['patch'=2,'epoch'=4,'tile'=4] {'epoch'}, dimensions={0}, use_global_device_ids=true | all-gather | bytes 245760 | tf_op jit(solution)/shard_map/all_gather | solution.py:168
  15.8 0.1 fusion
  15.9 1.3 %collective-permute-start = (f32[384,10]{1,0:T(8,128)S(1)}, f32[384,10]{1,0:T(8,128)S(1)}, u32[]{:S(2)}, u32[]{:S(2)}) collective-permute-start(f32[384,10]{1,0:T(8,128)S(1)} %get-tuple-element.9), channel_id=1, source_target_pairs={{1,0},{2,1},{3,2},{5,4},{6,5},{7,6},{9,8},{10,9},{11,10},{13,12},{... | collective-permute-start | bytes 46088 | tf_op jit(solution)/shard_map/ppermute | solution.py:169
  17.2 3.0 %collective-permute-start.1 = (f32[384,10]{1,0:T(8,128)S(1)}, f32[384,10]{1,0:T(8,128)S(1)}, u32[]{:S(2)}, u32[]{:S(2)}) collective-permute-start(f32[384,10]{1,0:T(8,128)S(1)} %get-tuple-element.10), channel_id=1, source_target_pairs={{0,1},{1,2},{2,3},{4,5},{5,6},{6,7},{8,9},{9,10},{10,11},{12,13},{... | collective-permute-start | bytes 46088 | tf_op jit(solution)/shard_map/ppermute | solution.py:170
  20.3 0.7 %pad.16.rowp_ref = f32[12,256]{1,0:T(8,128)S(1)} pad(f32[12,21]{1,0:T(8,128)} %param.9, f32[]{:T(128)} %constant.1.clone.1), padding=0_0x0_235 | pad | bytes 13300 | tf_op jit(solution)/shard_map/jit(_pad)/pad | solution.py:189
  21.0 0.7 %pad.17.colp_ref = f32[12,256]{1,0:T(8,128)S(1)} pad(f32[12,21]{1,0:T(8,128)} %param.10, f32[]{:T(128)} %constant.1.clone.1), padding=0_0x0_235 | pad | bytes 13300 | tf_op jit(solution)/shard_map/jit(_pad)/pad | solution.py:190
  21.7 0.7 %copy.8.cov_ref = s32[64,1]{1,0:T(8,128)S(1)} copy(s32[64,1]{0,1:T(1,128)} %bitcast.4) | data formatting | bytes 512 | tf_op jit(solution)/shard_map/reshape | solution.py:191
  22.4 0.7 %copy.9.scol_ref = s32[64,1]{1,0:T(8,128)S(1)} copy(s32[64,1]{0,1:T(1,128)} %bitcast.5) | data formatting | bytes 512 | tf_op jit(solution)/shard_map/reshape | solution.py:193
  23.2 0.1 pad.19.clone
  23.3 0.0 collective-permute-done
  23.3 0.0 collective-permute-done.1
  23.3 0.1 pad_maximum_fusion
  23.4 0.0 copy-done
  23.4 0.0 copy-done.1
  23.4 19.6 %shard_map.73 = (f32[12,384,128]{2,1,0:T(8,128)S(1)}, f32[48,48]{1,0:T(8,128)S(1)}) custom-call(f32[448,128]{1,0:T(8,128)S(1)} %pad.14.strip_ref, f32[448,128]{1,0:T(8,128)S(1)} %pad.15.side_ref, f32[1,384,128]{2,1,0:T(8,128)S(1)} %copy-done, f32[12,256]{1,0:T(8,128)S(1)} %pad.16.rowp_ref, f32[12,256]{1,0:T(8,128)S(1)} %pad.17.colp_ref, ...), custom_call_target="tpu_custom_call" | custom-call | tf_op jit(solution)/shard_map/pallas_call | solution.py:175
  43.1 11.2 %psum.7.gram_ref = f32[48,48]{1,0:T(8,128)S(1)} all-reduce(f32[48,48]{1,0:T(8,128)S(1)} %get-tuple-element.7), channel_id=1, replica_groups=mesh['patch'=2,'epoch'=4,'tile'=4] {'tile'}, use_global_device_ids=true, to_apply=%region_0.1 | all-reduce | flops 2304 | bytes 18432 | tf_op jit(solution)/shard_map/psum | solution.py:195
  54.3 4.6 %shard_map.74 = f32[1,384,128]{2,1,0:T(8,128)} custom-call(f32[48,48]{1,0:T(8,128)S(1)} %psum.7.gram_ref, f32[12,384,128]{2,1,0:T(8,128)S(1)} %get-tuple-element.8.images_ref, f32[1,384,128]{2,1,0:T(8,128)S(1)} %copy-done), custom_call_target="tpu_custom_call" | custom-call | tf_op jit(solution)/shard_map/pallas_call | solution.py:196
  (3 shorter events, 0.0 us)
Async XLA Ops:
  0.0 23.4 %copy-start = (f32[1,384,128]{2,1,0:T(8,128)S(1)}, f32[1,384,128]{2,1,0:T(8,128)}, u32[]{:S(2)}) copy-start(f32[1,384,128]{2,1,0:T(8,128)} %science_ref.3) | copy-start | bytes 589828
  0.0 23.4 %copy-start.1 = (s32[64]{0:T(128)S(1)}, s32[64]{0:T(128)}, u32[]{:S(2)}) copy-start(s32[64]{0:T(128)} %param.12) | copy-start | bytes 772
  15.9 7.4 %collective-permute-start = (f32[384,10]{1,0:T(8,128)S(1)}, f32[384,10]{1,0:T(8,128)S(1)}, u32[]{:S(2)}, u32[]{:S(2)}) collective-permute-start(f32[384,10]{1,0:T(8,128)S(1)} %get-tuple-element.9), channel_id=1, source_target_pairs={{1,0},{2,1},{3,2},{5,4},{6,5},{7,6},{9,8},{10,9},{11,10},{13,12},{... | collective-permute-start | bytes 46088 | tf_op jit(solution)/shard_map/ppermute | solution.py:169
  17.2 6.1 %collective-permute-start.1 = (f32[384,10]{1,0:T(8,128)S(1)}, f32[384,10]{1,0:T(8,128)S(1)}, u32[]{:S(2)}, u32[]{:S(2)}) collective-permute-start(f32[384,10]{1,0:T(8,128)S(1)} %get-tuple-element.10), channel_id=1, source_target_pairs={{0,1},{1,2},{2,3},{4,5},{5,6},{6,7},{8,9},{9,10},{10,11},{12,13},{... | collective-permute-start | bytes 46088 | tf_op jit(solution)/shard_map/ppermute | solution.py:170
where the time goes:
time: 59.2 us; the launch traced here: 58.9 us
  blocking collectives  27 us (46%)
  Pallas kernels  24.2 us (41%)
  starting transfers between devices  4.33 us (7%)
  local copies, waits for them, and re-layouts  3.13 us (5%)
    pallas_call x1, Pallas kernels, local(): pl.pallas_call(functools.partial(front, taps, total), out_shape=(jax.Shap...  19.6 us
    all_gather x1, blocking collectives, local(): column = lax.all_gather(template, 'epoch', axis=0, tiled=True)  15.8 us
    psum x1, blocking collectives, local(): normal = lax.psum(normal, 'tile')  11.2 us
    pallas_call x1, Pallas kernels, local(): pl.pallas_call(functools.partial(back, total), out_shape=jax.ShapeDtypeSt...  4.61 us
    ppermute x1, starting transfers between devices, local(): lax.ppermute(column[:, cols - half:], 'tile', [(i, i + 1) for i in range(...  3.04 us
    ppermute x1, starting transfers between devices, local(): lax.ppermute(column[:, :half], 'tile', [(i + 1, i) for i in range(tiles -...  1.29 us
  transfers between devices with their start and end apart: 2, of which 0 were waited for; matrix products, arithmetic and copies ran while one was open for 5% of the time, Pallas kernels for 0%

commit v1 on v0

v1 whole, which is shorter than its diff:
```python
import functools

import jax
import jax.numpy as jnp
from jax import lax
from jax.experimental import pallas as pl
from jax.experimental.pallas import tpu as pltpu
from jax.sharding import PartitionSpec as P

S = 32
GROUP = 16
EDGE = 16
CHUNK = 16
LANES = 128
ridge_weight = 1.0
F32 = jnp.float32
BF16 = jnp.bfloat16
NT = (((1,), (1,)), ((), ()))
NN = (((1,), (0,)), ((), ()))


def split(value):
    high = value.astype(BF16)
    return high, (value - high.astype(F32)).astype(BF16)


def dot3(left, right, dims):
    left_high, left_low = left
    right_high, right_low = right
    dot = functools.partial(lax.dot_general, dimension_numbers=dims, preferred_element_type=F32)
    return dot(left_high, right_high) + (dot(left_high, right_low) + dot(left_low, right_high))


def toeplitz(profile_row, rows, shift, width):
    base = pltpu.roll(jnp.broadcast_to(profile_row, (8, width)), 0, 1, stride=1, stride_axis=0)
    turns = [(shift + first) % width for first in range(0, rows, 8)]
    return jnp.concatenate([pltpu.roll(base, turn, 1) if turn else base for turn in turns], axis=0)


def iota(shape, axis):
    return lax.broadcasted_iota(jnp.int32, shape, axis)


def row_block(rows, extra, width):
    best = 8
    for size in range(8, width - extra + 1, 8):
        if rows % size == 0:
            best = size
    return best


def xi_row(cols, total):
    start = lax.axis_index("tile") * cols
    return 2.0 * (start + iota((1, cols), 1)).astype(F32) / total - 1.0


def make_bands(rowp_ref, colp_ref, profile_ref, row_band_ref, col_band_ref, shift):
    count, taps = rowp_ref.shape
    width = profile_ref.shape[2]
    profile_ref[...] = jnp.zeros_like(profile_ref)
    profile_ref[0, :count, :taps] = rowp_ref[...]
    profile_ref[1, :count, :taps] = colp_ref[...]
    for b in range(count):
        band = split(toeplitz(profile_ref[0, b : b + 1, :], row_band_ref.shape[2], shift, width))
        row_band_ref[0, b], row_band_ref[1, b] = band
        band = split(toeplitz(profile_ref[1, b : b + 1, :], col_band_ref.shape[2], -(taps // 2), width))
        col_band_ref[0, b], col_band_ref[1, b] = band


def convolve(strip, row_band_ref, col_band_ref, images_ref, mixed_ref):
    count, rows, cols = images_ref.shape
    block, width = row_band_ref.shape[2:]
    strip = split(strip)
    for b in range(count):
        across = dot3(strip, (col_band_ref[0, b], col_band_ref[1, b]), NT)
        across = split(across)
        band = (row_band_ref[0, b], row_band_ref[1, b])
        for start in range(0, rows, block):
            piece = dot3(band, tuple(part[start : start + width] for part in across), NN)
            images_ref[b, start : start + block, :] = piece
            mixed_ref[pl.ds(start * GROUP + b, block, stride=GROUP), :] = piece


def make_weight(srow_ref, scol_ref, cov_ref, weight_ref):
    cols = weight_ref.shape[1]
    stamps = srow_ref.shape[1]
    at = iota((cols, stamps), 0) - scol_ref[...]
    cols_in = jnp.where((at >= 0) & (at < S), cov_ref[...].astype(F32), 0.0).astype(BF16)
    size = CHUNK * GROUP

    def body(chunk, carry):
        at_row = chunk * CHUNK + iota((size, 1), 0) // GROUP - srow_ref[...]
        rows_in = jnp.where((at_row >= 0) & (at_row < S), 1.0, 0.0).astype(BF16)
        at = pl.ds(pl.multiple_of(chunk * size, size), size)
        weight_ref[at, :] = lax.dot_general(rows_in, cols_in, NT, preferred_element_type=F32)
        return carry

    lax.fori_loop(0, weight_ref.shape[0] // size, body, 0)


def gram(weight_ref, mixed_ref, total):
    height, cols = mixed_ref.shape
    rows = height // GROUP
    xi = xi_row(cols, total)
    size = CHUNK * GROUP

    def lay(values):
        return jnp.concatenate(
            [
                jnp.concatenate([v[k * GROUP : (k + 1) * GROUP] for k in range(CHUNK)], axis=1)
                for v in values
            ],
            axis=0,
        )

    def body(chunk, acc):
        at = pl.ds(pl.multiple_of(chunk * size, size), size)
        base = mixed_ref[at, :]
        weight = weight_ref[at, :]
        y = chunk * CHUNK + iota((size, 1), 0) // GROUP
        eta = 2.0 * y.astype(F32) / rows - 1.0
        feats = (base, base * xi, base * eta)
        right = split(lay(feats))
        left = split(lay([f * weight for f in feats]))
        return acc + dot3(left, right, NT)

    return lax.fori_loop(0, rows // CHUNK, body, jnp.zeros((3 * GROUP, 3 * GROUP), F32))


def solve(normal, count):
    side = 3 * GROUP
    row, col = iota((side, LANES), 0), iota((side, LANES), 1)

    def used(k):
        return ((k % GROUP < count) & (k < side)) | (k == count)

    rhs = normal[:, count + 1 : count + 2]
    system = jnp.where(used(row) & used(col), normal, 0.0) + ridge_weight * jnp.where(row == col, 1.0, 0.0)
    system = jnp.where((col == side) & used(row), rhs, system)
    unknowns = [k for k in range(side) if (k % GROUP < count) or k == count]
    for p in unknowns:
        pivot_row = system[p : p + 1, :]
        factor = system[:, p : p + 1] / system[p : p + 1, p : p + 1]
        factor = jnp.where(row[:, :1] == p, 0.0, factor)
        system = system - factor * pivot_row
    diagonal = jnp.sum(jnp.where(row == col, system, 0.0), axis=1, keepdims=True)
    return system[:, side : side + 1] / diagonal


def apply(coefs, images_ref, science_ref, out_ref, total):
    count, rows, cols = images_ref.shape
    xi = xi_row(cols, total)
    eta = 2.0 * iota((rows, 1), 0).astype(F32) / rows - 1.0
    field = jnp.broadcast_to(coefs[count : count + 1, :], (rows, cols))
    for b in range(count):
        flat = coefs[b : b + 1] + coefs[GROUP + b : GROUP + b + 1] * xi
        field = field + images_ref[b] * (flat + coefs[2 * GROUP + b : 2 * GROUP + b + 1] * eta)
    out_ref[0] = science_ref[0] - field


def fill_rest(mixed_ref, science, count):
    rows = science.shape[0]
    mixed_ref[pl.ds(count, rows, stride=GROUP), :] = jnp.ones_like(science)
    mixed_ref[pl.ds(count + 1, rows, stride=GROUP), :] = science
    for spare in range(count + 2, GROUP):
        mixed_ref[pl.ds(spare, rows, stride=GROUP), :] = jnp.zeros_like(science)


def remote(source, target, send, recv, epoch, tile):
    return pltpu.make_async_remote_copy(
        src_ref=source,
        dst_ref=target,
        send_sem=send,
        recv_sem=recv,
        device_id={"epoch": epoch, "tile": tile},
        device_id_type=pl.DeviceIdType.MESH,
    )


def kernel(total, top, template_ref, science_ref, rowp_ref, colp_ref, cov_ref, srow_ref, scol_ref, out_ref,
           slots, pack, edges, strip, parts, mine, images_ref, mixed_ref, weight_ref, profile_ref,
           row_band_ref, col_band_ref, slot_send, slot_recv, edge_send, edge_recv, part_send, part_recv):
    count, rows, cols = images_ref.shape
    taps = rowp_ref.shape[1]
    epochs, own_rows, _ = slots.shape
    tiles = parts.shape[0]
    epoch, tile = lax.axis_index("epoch"), lax.axis_index("tile")

    flipped = jnp.transpose(template_ref[...])
    pack[0] = flipped[:EDGE]
    pack[1] = flipped[cols - EDGE :]
    slots[epoch] = template_ref[...]

    barrier = pltpu.get_barrier_semaphore()
    for e in range(epochs):
        for t in range(tiles):
            if e or t:
                where = {"epoch": lax.rem(epoch + e, epochs), "tile": lax.rem(tile + t, tiles)}
                pl.semaphore_signal(barrier, inc=1, device_id=where, device_id_type=pl.DeviceIdType.MESH)
    pl.semaphore_wait(barrier, epochs * tiles - 1)

    def block_copy(e, source):
        return remote(template_ref, slots.at[source], slot_send.at[e], slot_recv.at[source],
                      lax.rem(epoch + e, epochs), tile)

    def edge_copy(e, side, source):
        beside = tile - 1 if side == 0 else tile + 1
        return remote(pack.at[side], edges.at[side, source], edge_send.at[side, e], edge_recv.at[side, source],
                      lax.rem(epoch + e, epochs), beside)

    has_left, has_right = tile > 0, tile < tiles - 1
    order = sorted(range(epochs), key=lambda e: -e * (epochs - e))
    for e in order:
        if e:
            block_copy(e, epoch).start()

        @pl.when(has_left)
        def _():
            edge_copy(e, 0, epoch).start()

        @pl.when(has_right)
        def _():
            edge_copy(e, 1, epoch).start()

    fill_rest(mixed_ref, science_ref[0], count)
    make_weight(srow_ref, scol_ref, cov_ref, weight_ref)
    make_bands(rowp_ref, colp_ref, profile_ref, row_band_ref, col_band_ref, top - taps // 2)
    strip[...] = jnp.zeros_like(strip)

    @pl.when(tile == tiles - 1)
    def _():
        edges[0] = jnp.zeros(edges.shape[1:], F32)

    @pl.when(tile == 0)
    def _():
        edges[1] = jnp.zeros(edges.shape[1:], F32)

    for e in range(epochs):
        source = lax.rem(epoch + epochs - e, epochs)
        if e:
            block_copy(e, source).wait_recv()
            block_copy(e, epoch).wait_send()

        @pl.when(has_left)
        def _():
            edge_copy(e, 0, epoch).wait_send()
            edge_copy(e, 1, source).wait_recv()

        @pl.when(has_right)
        def _():
            edge_copy(e, 1, epoch).wait_send()
            edge_copy(e, 0, source).wait_recv()

    middle = jnp.zeros((cols - 2 * EDGE, own_rows), F32)
    for e in range(epochs):
        at = pl.ds(top + e * own_rows, own_rows)
        strip[at, :cols] = slots[e]
        strip[at, cols:] = jnp.transpose(jnp.concatenate([edges[0, e], middle, edges[1, e]], axis=0))
    convolve(strip[...], row_band_ref, col_band_ref, images_ref, mixed_ref)
    normal = gram(weight_ref, mixed_ref, total)
    side = 3 * GROUP
    normal = jnp.concatenate([normal, jnp.zeros((side, LANES - side), F32)], axis=1)
    mine[...] = normal

    def part_copy(t, source):
        return remote(mine, parts.at[source], part_send.at[t], part_recv.at[source],
                      epoch, lax.rem(tile + t, tiles))

    for t in range(1, tiles):
        part_copy(t, tile).start()
    for t in range(1, tiles):
        source = lax.rem(tile + tiles - t, tiles)
        part_copy(t, source).wait_recv()
        normal = normal + parts[source]
    for t in range(1, tiles):
        part_copy(t, tile).wait_send()
    coefs = solve(normal, count)
    apply(coefs, images_ref, science_ref, out_ref, total)


def local(template, science, row_profiles, col_profiles, coverage, stamp_rows, stamp_cols):
    count, taps = row_profiles.shape
    rows, cols = science.shape[1:]
    own_rows = template.shape[0]
    tiles, epochs = lax.axis_size("tile"), lax.axis_size("epoch")
    width = 2 * LANES
    top = -(-(taps // 2) // 8) * 8
    block = row_block(rows, taps - 1 + top - taps // 2, width)
    vmem = pl.BlockSpec(memory_space=pltpu.VMEM)
    dma = pltpu.SemaphoreType.DMA
    return pl.pallas_call(
        functools.partial(kernel, cols * tiles, top),
        out_shape=jax.ShapeDtypeStruct(science.shape, F32),
        in_specs=[vmem] * 7,
        out_specs=vmem,
        scratch_shapes=[
            pltpu.VMEM((epochs, own_rows, cols), F32),
            pltpu.VMEM((2, EDGE, own_rows), F32),
            pltpu.VMEM((2, epochs, EDGE, own_rows), F32),
            pltpu.VMEM((rows - block + width, width), F32),
            pltpu.VMEM((tiles, 3 * GROUP, LANES), F32),
            pltpu.VMEM((3 * GROUP, LANES), F32),
            pltpu.VMEM((count, rows, cols), F32),
            pltpu.VMEM((rows * GROUP, cols), F32),
            pltpu.VMEM((rows * GROUP, cols), F32),
            pltpu.VMEM((2, GROUP, width), F32),
            pltpu.VMEM((2, count, block, width), BF16),
            pltpu.VMEM((2, count, cols, width), BF16),
            dma((epochs,)),
            dma((epochs,)),
            dma((2, epochs)),
            dma((2, epochs)),
            dma((tiles,)),
            dma((tiles,)),
        ],
        compiler_params=pltpu.CompilerParams(
            collective_id=0, has_side_effects=True, vmem_limit_bytes=48 * 2**20
        ),
    )(
        template,
        science,
        row_profiles,
        col_profiles,
        coverage,
        stamp_rows.reshape(1, -1),
        stamp_cols.reshape(1, -1),
    )


def solution(mesh):
    in_specs = (
        P(("patch", "epoch"), "tile"),
        P(("patch", "epoch"), None, "tile"),
        P(),
        P(),
        P(("patch", "epoch"), "tile"),
        P(("patch", "tile")),
        P(("patch", "tile")),
    )
    out_specs = P(("patch", "epoch"), None, "tile")
    return jax.shard_map(local, mesh=mesh, in_specs=in_specs, out_specs=out_specs, check_vma=False)
```

time: 59.2 us -> 41.6 us (0.70)
  blocking collectives: 27 us -> 0 us
  Pallas kernels: 24.2 us -> 36.8 us
  starting transfers between devices: 4.33 us -> 0 us
  local copies, waits for them, and re-layouts: 3.13 us -> 4.48 us
    all_gather x1 -> x0, blocking collectives: 15.8 us -> none  [local(): column = lax.all_gather(template, 'epoch', axis=0, tiled=True)]
    pallas_call x2 -> x1, Pallas kernels: 24.2 us -> 36.8 us  [local(): pl.pallas_call(functools.partial(kernel, cols * tiles, top), out_shape=ja...]
    psum x1 -> x0, blocking collectives: 11.2 us -> none  [local(): normal = lax.psum(normal, 'tile')]
    unnamed x4 -> x15, local copies, waits for them, and re-layouts: 0.01 us -> 4.48 us
    ppermute x2 -> x0, starting transfers between devices: 4.33 us -> none  [the longest x1 3.04 us: local(): lax.ppermute(column[:, cols - half:], 'tile', [(i, i + 1) for i in range(...]
    reshape x2 -> x0, local copies, waits for them, and re-layouts: 1.49 us -> none  [the longest x1 0.74 us: local(): coverage.reshape(-1, 1)]
    pad x4 -> x0, local copies, waits for them, and re-layouts: 1.44 us -> none  [the longest x1 0.71 us: local(): jnp.pad(row_profiles, fit)]
  transfers between devices with their start and end apart: 2 -> 0, of which waited for: 0 -> 0; matrix products, arithmetic and copies ran while one was open for 5% -> 0% of each run, Pallas kernels for 0% -> 0%
where the time goes in v1:
time: 41.6 us; the launch traced here: 41.3 us
  Pallas kernels  36.8 us (88%)
  local copies, waits for them, and re-layouts  4.48 us (11%)
    pallas_call x1, Pallas kernels, local(): pl.pallas_call(functools.partial(kernel, cols * tiles, top), out_shape=ja...  36.8 us
    unnamed x15, local copies, waits for them, and re-layouts  4.48 us

profile of v1, /device:TPU:0, one launch (start us, length us, event | category | flops | bytes accessed | tf_op | source)
XLA Modules:
  0.0 41.3 jit_solution(1277866114103285659)
XLA Ops:
  0.0 0.0 copy-start.4
  0.0 0.0 copy-start.5
  0.0 0.0 copy-start.6
  0.0 0.6 %copy-done.4 = s32[1,64]{1,0:T(1,128)S(1)} copy-done((s32[1,64]{1,0:T(1,128)S(1)}, s32[1,64]{1,0:T(1,128)}, u32[]{:S(2)}) %copy-start.4) | copy-done | bytes 280
  0.7 0.0 copy-done.5
  0.7 0.0 copy-done.6
  0.7 0.0 copy-start
  0.7 0.9 %copy-done = f32[1,384,128]{2,1,0:T(8,128)S(1)} copy-done((f32[1,384,128]{2,1,0:T(8,128)S(1)}, f32[1,384,128]{2,1,0:T(8,128)}, u32[]{:S(2)}) %copy-start) | copy-done | bytes 196632
  1.6 0.0 copy-start.1
  1.6 0.8 %copy-done.1 = f32[96,128]{1,0:T(8,128)S(1)} copy-done((f32[96,128]{1,0:T(8,128)S(1)}, f32[96,128]{1,0:T(8,128)}, u32[]{:S(2)}) %copy-start.1) | copy-done | bytes 49176
  2.4 0.0 copy-start.2
  2.4 0.7 %copy-done.2 = f32[12,21]{1,0:T(8,128)S(1)} copy-done((f32[12,21]{1,0:T(8,128)S(1)}, f32[12,21]{1,0:T(8,128)}, u32[]{:S(2)}) %copy-start.2) | copy-done | bytes 1032
  3.1 0.0 copy-start.3
  3.1 0.7 %copy-done.3 = f32[12,21]{1,0:T(8,128)S(1)} copy-done((f32[12,21]{1,0:T(8,128)S(1)}, f32[12,21]{1,0:T(8,128)}, u32[]{:S(2)}) %copy-start.3) | copy-done | bytes 1032
  3.8 36.8 %shard_map.73 = f32[1,384,128]{2,1,0:T(8,128)S(1)} custom-call(f32[96,128]{1,0:T(8,128)S(1)} %copy-done.1, f32[1,384,128]{2,1,0:T(8,128)S(1)} %copy-done, f32[12,21]{1,0:T(8,128)S(1)} %copy-done.2, f32[12,21]{1,0:T(8,128)S(1)} %copy-done.3, s32[1,64]{1,0:T(1,128)S(1)} %copy-done.4, s32[1,64]{1,0:T(1,128)S(1)} %bitcast.2, s32[1,64]{1,0:T(1,128)S(1)} %bitcast.3), custom_call_target="tpu_custom_call" | custom-call | tf_op jit(solution)/shard_map/pallas_call | solution.py:291
  40.7 0.7 %copy.9 = f32[1,384,128]{2,1,0:T(8,128)} copy(f32[1,384,128]{2,1,0:T(8,128)S(1)} %shard_map.73) | data formatting | bytes 393216
Async XLA Ops:
  0.0 0.7 %copy-start.4 = (s32[1,64]{1,0:T(1,128)S(1)}, s32[1,64]{1,0:T(1,128)}, u32[]{:S(2)}) copy-start(s32[1,64]{1,0:T(1,128)} %cov_ref.1) | copy-start | bytes 772
  0.0 0.7 %copy-start.5 = (s32[64]{0:T(128)S(1)}, s32[64]{0:T(128)}, u32[]{:S(2)}) copy-start(s32[64]{0:T(128)} %param.12) | copy-start | bytes 772
  0.0 0.7 %copy-start.6 = (s32[64]{0:T(128)S(1)}, s32[64]{0:T(128)}, u32[]{:S(2)}) copy-start(s32[64]{0:T(128)} %param.13) | copy-start | bytes 772
  0.7 0.9 %copy-start = (f32[1,384,128]{2,1,0:T(8,128)S(1)}, f32[1,384,128]{2,1,0:T(8,128)}, u32[]{:S(2)}) copy-start(f32[1,384,128]{2,1,0:T(8,128)} %science_ref.1) | copy-start | bytes 589828
  1.6 0.8 %copy-start.1 = (f32[96,128]{1,0:T(8,128)S(1)}, f32[96,128]{1,0:T(8,128)}, u32[]{:S(2)}) copy-start(f32[96,128]{1,0:T(8,128)} %template_ref.1) | copy-start | bytes 147460
  2.4 0.7 %copy-start.2 = (f32[12,21]{1,0:T(8,128)S(1)}, f32[12,21]{1,0:T(8,128)}, u32[]{:S(2)}) copy-start(f32[12,21]{1,0:T(8,128)} %rowp_ref.1) | copy-start | bytes 3028
  3.1 0.7 %copy-start.3 = (f32[12,21]{1,0:T(8,128)S(1)}, f32[12,21]{1,0:T(8,128)}, u32[]{:S(2)}) copy-start(f32[12,21]{1,0:T(8,128)} %colp_ref.1) | copy-start | bytes 3028

commit v2 on v1

--- a/solution.py
+++ b/solution.py
@@ -11,6 +11,7 @@
 GROUP = 16
 EDGE = 16
 CHUNK = 16
+UNROLL = 2
 LANES = 128
 ridge_weight = 1.0
 F32 = jnp.float32
@@ -22,13 +23,6 @@
 def split(value):
     high = value.astype(BF16)
     return high, (value - high.astype(F32)).astype(BF16)
-
-
-def dot3(left, right, dims):
-    left_high, left_low = left
-    right_high, right_low = right
-    dot = functools.partial(lax.dot_general, dimension_numbers=dims, preferred_element_type=F32)
-    return dot(left_high, right_high) + (dot(left_high, right_low) + dot(left_low, right_high))
 
 
 def toeplitz(profile_row, rows, shift, width):
@@ -67,16 +61,30 @@
         col_band_ref[0, b], col_band_ref[1, b] = band
 
 
-def convolve(strip, row_band_ref, col_band_ref, images_ref, mixed_ref):
+def column_pass(strip, at, col_band_ref, across_ref):
+    count, _, lanes = across_ref.shape
+    cols = lanes // 2
+    high, low = split(strip)
+    dot = functools.partial(lax.dot_general, dimension_numbers=NT, preferred_element_type=F32)
+    for pair in range(0, count, 2):
+        members = [b for b in (pair, pair + 1) if b < count]
+        small = dot(low, jnp.concatenate([col_band_ref[0, b] for b in members], axis=0))
+        for k, b in enumerate(members):
+            big = dot(high, jnp.concatenate([col_band_ref[0, b], col_band_ref[1, b]], axis=0))
+            across = big[:, :cols] + (big[:, cols:] + small[:, k * cols : (k + 1) * cols])
+            across_ref[b, at, :] = jnp.concatenate(split(across), axis=1)
+
+
+def row_pass(row_band_ref, across_ref, images_ref, mixed_ref):
     count, rows, cols = images_ref.shape
     block, width = row_band_ref.shape[2:]
-    strip = split(strip)
+    dot = functools.partial(lax.dot_general, dimension_numbers=NN, preferred_element_type=F32)
     for b in range(count):
-        across = dot3(strip, (col_band_ref[0, b], col_band_ref[1, b]), NT)
-        across = split(across)
-        band = (row_band_ref[0, b], row_band_ref[1, b])
         for start in range(0, rows, block):
-            piece = dot3(band, tuple(part[start : start + width] for part in across), NN)
+            across = across_ref[b, start : start + width, :]
+            big = dot(row_band_ref[0, b], across)
+            small = dot(row_band_ref[1, b], across[:, :cols])
+            piece = big[:, :cols] + (big[:, cols:] + small)
             images_ref[b, start : start + block, :] = piece
             mixed_ref[pl.ds(start * GROUP + b, block, stride=GROUP), :] = piece
 
@@ -120,11 +128,13 @@
         y = chunk * CHUNK + iota((size, 1), 0) // GROUP
         eta = 2.0 * y.astype(F32) / rows - 1.0
         feats = (base, base * xi, base * eta)
-        right = split(lay(feats))
-        left = split(lay([f * weight for f in feats]))
-        return acc + dot3(left, right, NT)
-
-    return lax.fori_loop(0, rows // CHUNK, body, jnp.zeros((3 * GROUP, 3 * GROUP), F32))
+        right = jnp.concatenate(split(lay(feats)), axis=0)
+        left = jnp.concatenate(split(lay([f * weight for f in feats])), axis=0)
+        return acc + lax.dot_general(left, right, NT, preferred_element_type=F32)
+
+    side = 3 * GROUP
+    sums = lax.fori_loop(0, rows // CHUNK, body, jnp.zeros((2 * side, 2 * side), F32), unroll=UNROLL)
+    return sums[:side, :side] + (sums[:side, side:] + sums[side:, :side] + sums[side:, side:])
 
 
 def solve(normal, count):
@@ -177,30 +187,49 @@
     )
 
 
-def kernel(total, top, template_ref, science_ref, rowp_ref, colp_ref, cov_ref, srow_ref, scol_ref, out_ref,
-           slots, pack, edges, strip, parts, mine, images_ref, mixed_ref, weight_ref, profile_ref,
-           row_band_ref, col_band_ref, slot_send, slot_recv, edge_send, edge_recv, part_send, part_recv):
+def kernel(total, top, template_in, science_in, rowp_in, colp_in, cov_in, srow_in, scol_in, out_ref,
+           science_ref, rowp_ref, colp_ref, cov_ref, srow_ref, scol_ref,
+           slots, pack, edges, across_ref, parts, mine, images_ref, mixed_ref, weight_ref, profile_ref,
+           row_band_ref, col_band_ref, slot_send, slot_recv, edge_send, edge_recv, part_send, part_recv, load_sem):
     count, rows, cols = images_ref.shape
     taps = rowp_ref.shape[1]
     epochs, own_rows, _ = slots.shape
     tiles = parts.shape[0]
     epoch, tile = lax.axis_index("epoch"), lax.axis_index("tile")
 
-    flipped = jnp.transpose(template_ref[...])
-    pack[0] = flipped[:EDGE]
-    pack[1] = flipped[cols - EDGE :]
-    slots[epoch] = template_ref[...]
-
+    loads = [
+        pltpu.make_async_copy(source, target, load_sem.at[k])
+        for k, (source, target) in enumerate(
+            [
+                (template_in, slots.at[epoch]),
+                (cov_in, cov_ref),
+                (srow_in, srow_ref),
+                (scol_in, scol_ref),
+                (rowp_in, rowp_ref),
+                (colp_in, colp_ref),
+                (science_in, science_ref),
+            ]
+        )
+    ]
+    for load in loads:
+        load.start()
     barrier = pltpu.get_barrier_semaphore()
     for e in range(epochs):
         for t in range(tiles):
             if e or t:
                 where = {"epoch": lax.rem(epoch + e, epochs), "tile": lax.rem(tile + t, tiles)}
                 pl.semaphore_signal(barrier, inc=1, device_id=where, device_id_type=pl.DeviceIdType.MESH)
+    loads[0].wait()
+    flipped = jnp.transpose(slots[epoch])
+    pack[0] = flipped[:EDGE]
+    pack[1] = flipped[cols - EDGE :]
+    for load in loads[1:4]:
+        load.wait()
+    make_weight(srow_ref, scol_ref, cov_ref, weight_ref)
     pl.semaphore_wait(barrier, epochs * tiles - 1)
 
     def block_copy(e, source):
-        return remote(template_ref, slots.at[source], slot_send.at[e], slot_recv.at[source],
+        return remote(slots.at[epoch], slots.at[source], slot_send.at[e], slot_recv.at[source],
                       lax.rem(epoch + e, epochs), tile)
 
     def edge_copy(e, side, source):
@@ -222,10 +251,13 @@
         def _():
             edge_copy(e, 1, epoch).start()
 
+    for load in loads[4:]:
+        load.wait()
+    make_bands(rowp_ref, colp_ref, profile_ref, row_band_ref, col_band_ref, top - taps // 2)
     fill_rest(mixed_ref, science_ref[0], count)
-    make_weight(srow_ref, scol_ref, cov_ref, weight_ref)
-    make_bands(rowp_ref, colp_ref, profile_ref, row_band_ref, col_band_ref, top - taps // 2)
-    strip[...] = jnp.zeros_like(strip)
+    high = across_ref.shape[1]
+    across_ref[:, :top, :] = jnp.zeros((count, top, 2 * cols), BF16)
+    across_ref[:, top + rows :, :] = jnp.zeros((count, high - top - rows, 2 * cols), BF16)
 
     @pl.when(tile == tiles - 1)
     def _():
@@ -235,28 +267,38 @@
     def _():
         edges[1] = jnp.zeros(edges.shape[1:], F32)
 
-    for e in range(epochs):
-        source = lax.rem(epoch + epochs - e, epochs)
-        if e:
+    def arrive(source):
+        e = lax.rem(epoch + epochs - source, epochs)
+
+        @pl.when(e != 0)
+        def _():
             block_copy(e, source).wait_recv()
-            block_copy(e, epoch).wait_send()
 
         @pl.when(has_left)
         def _():
-            edge_copy(e, 0, epoch).wait_send()
             edge_copy(e, 1, source).wait_recv()
 
         @pl.when(has_right)
         def _():
-            edge_copy(e, 1, epoch).wait_send()
             edge_copy(e, 0, source).wait_recv()
 
     middle = jnp.zeros((cols - 2 * EDGE, own_rows), F32)
-    for e in range(epochs):
-        at = pl.ds(top + e * own_rows, own_rows)
-        strip[at, :cols] = slots[e]
-        strip[at, cols:] = jnp.transpose(jnp.concatenate([edges[0, e], middle, edges[1, e]], axis=0))
-    convolve(strip[...], row_band_ref, col_band_ref, images_ref, mixed_ref)
+
+    def strip_of(source):
+        beside = jnp.transpose(jnp.concatenate([edges[0, source], middle, edges[1, source]], axis=0))
+        return jnp.concatenate([slots[source], beside], axis=1)
+
+    groups = 2 if epochs % 2 == 0 and own_rows % 16 == 0 else 1
+    each = epochs // groups
+    for turn in range(groups):
+        group = lax.rem(epoch // each + turn, groups)
+        for k in range(each):
+            arrive(group * each + k)
+        strip = jnp.concatenate([strip_of(group * each + k) for k in range(each)], axis=0)
+        height = each * own_rows
+        at = pl.ds(pl.multiple_of(top + group * height, 16), height) if groups > 1 else pl.ds(top, height)
+        column_pass(strip, at, col_band_ref, across_ref)
+    row_pass(row_band_ref, across_ref, images_ref, mixed_ref)
     normal = gram(weight_ref, mixed_ref, total)
     side = 3 * GROUP
     normal = jnp.concatenate([normal, jnp.zeros((side, LANES - side), F32)], axis=1)
@@ -274,6 +316,18 @@
         normal = normal + parts[source]
     for t in range(1, tiles):
         part_copy(t, tile).wait_send()
+    for e in range(epochs):
+        if e:
+            block_copy(e, epoch).wait_send()
+
+        @pl.when(has_left)
+        def _():
+            edge_copy(e, 0, epoch).wait_send()
+
+        @pl.when(has_right)
+        def _():
+            edge_copy(e, 1, epoch).wait_send()
+
     coefs = solve(normal, count)
     apply(coefs, images_ref, science_ref, out_ref, total)
 
@@ -284,20 +338,26 @@
     own_rows = template.shape[0]
     tiles, epochs = lax.axis_size("tile"), lax.axis_size("epoch")
     width = 2 * LANES
-    top = -(-(taps // 2) // 8) * 8
+    top = -(-(taps // 2) // 16) * 16
     block = row_block(rows, taps - 1 + top - taps // 2, width)
     vmem = pl.BlockSpec(memory_space=pltpu.VMEM)
     dma = pltpu.SemaphoreType.DMA
     return pl.pallas_call(
         functools.partial(kernel, cols * tiles, top),
         out_shape=jax.ShapeDtypeStruct(science.shape, F32),
-        in_specs=[vmem] * 7,
+        in_specs=[pl.BlockSpec(memory_space=pl.ANY)] * 7,
         out_specs=vmem,
         scratch_shapes=[
+            pltpu.VMEM(science.shape, F32),
+            pltpu.VMEM(row_profiles.shape, F32),
+            pltpu.VMEM(col_profiles.shape, F32),
+            pltpu.VMEM(coverage.shape, jnp.int32),
+            pltpu.VMEM((1, stamp_rows.shape[0]), jnp.int32),
+            pltpu.VMEM((1, stamp_cols.shape[0]), jnp.int32),
             pltpu.VMEM((epochs, own_rows, cols), F32),
             pltpu.VMEM((2, EDGE, own_rows), F32),
             pltpu.VMEM((2, epochs, EDGE, own_rows), F32),
-            pltpu.VMEM((rows - block + width, width), F32),
+            pltpu.VMEM((count, rows - block + width, 2 * cols), BF16),
             pltpu.VMEM((tiles, 3 * GROUP, LANES), F32),
             pltpu.VMEM((3 * GROUP, LANES), F32),
             pltpu.VMEM((count, rows, cols), F32),
@@ -312,9 +372,10 @@
             dma((2, epochs)),
             dma((tiles,)),
             dma((tiles,)),
+            dma((7,)),
         ],
         compiler_params=pltpu.CompilerParams(
-            collective_id=0, has_side_effects=True, vmem_limit_bytes=48 * 2**20
+            collective_id=0, has_side_effects=True, vmem_limit_bytes=63 * 2**20
         ),
     )(
         template,

time: 41.6 us -> 31.9 us (0.77)
  Pallas kernels: 36.8 us -> 30.1 us
  local copies, waits for them, and re-layouts: 4.48 us -> 1.62 us
    pallas_call x1, Pallas kernels: 36.8 us -> 30.1 us  [local(): pl.pallas_call(functools.partial(kernel, cols * tiles, top), out_shape=ja...]
    unnamed x15 -> x1, local copies, waits for them, and re-layouts: 4.48 us -> 1.62 us
where the time goes in v2:
time: 31.9 us; the launch traced here: 31.7 us
  Pallas kernels  30.1 us (94%)
  local copies, waits for them, and re-layouts  1.62 us (5%)
    pallas_call x1, Pallas kernels, local(): pl.pallas_call(functools.partial(kernel, cols * tiles, top), out_shape=ja...  30.1 us
    unnamed x1, local copies, waits for them, and re-layouts  1.62 us

profile of v2, /device:TPU:0, one launch (start us, length us, event | category | flops | bytes accessed | tf_op | source)
XLA Modules:
  0.0 31.7 jit_solution(5344807154171479025)
XLA Ops:
  0.0 30.1 %shard_map.73 = f32[1,384,128]{2,1,0:T(8,128)} custom-call(f32[96,128]{1,0:T(8,128)} %template_in.1, f32[1,384,128]{2,1,0:T(8,128)} %science_in.1, f32[12,21]{1,0:T(8,128)} %rowp_in.1, f32[12,21]{1,0:T(8,128)} %colp_in.1, s32[1,64]{1,0:T(1,128)} %cov_in.1, s32[1,64]{1,0:T(1,128)} %bitcast.2, s32[1,64]{1,0:T(1,128)} %bitcast.3), custom_call_target="tpu_custom_call" | custom-call | tf_op jit(solution)/shard_map/pallas_call | solution.py:345
  30.1 1.6 %copy.9 = f32[1,384,128]{2,1,0:T(8,128)} copy(f32[1,384,128]{2,1,0:T(8,128)} %shard_map.73) | data formatting | bytes 393216

commit v3 on v2

--- a/solution.py
+++ b/solution.py
@@ -10,8 +10,7 @@
 S = 32
 GROUP = 16
 EDGE = 16
-CHUNK = 16
-UNROLL = 2
+CHUNK = 64
 LANES = 128
 ridge_weight = 1.0
 F32 = jnp.float32
@@ -89,15 +88,20 @@
             mixed_ref[pl.ds(start * GROUP + b, block, stride=GROUP), :] = piece
 
 
+def chunk_rows(rows):
+    return max(size for size in range(1, CHUNK + 1) if rows % size == 0)
+
+
 def make_weight(srow_ref, scol_ref, cov_ref, weight_ref):
     cols = weight_ref.shape[1]
     stamps = srow_ref.shape[1]
     at = iota((cols, stamps), 0) - scol_ref[...]
     cols_in = jnp.where((at >= 0) & (at < S), cov_ref[...].astype(F32), 0.0).astype(BF16)
-    size = CHUNK * GROUP
+    step = chunk_rows(weight_ref.shape[0] // GROUP)
+    size = step * GROUP
 
     def body(chunk, carry):
-        at_row = chunk * CHUNK + iota((size, 1), 0) // GROUP - srow_ref[...]
+        at_row = chunk * step + iota((size, 1), 0) // GROUP - srow_ref[...]
         rows_in = jnp.where((at_row >= 0) & (at_row < S), 1.0, 0.0).astype(BF16)
         at = pl.ds(pl.multiple_of(chunk * size, size), size)
         weight_ref[at, :] = lax.dot_general(rows_in, cols_in, NT, preferred_element_type=F32)
@@ -110,12 +114,13 @@
     height, cols = mixed_ref.shape
     rows = height // GROUP
     xi = xi_row(cols, total)
-    size = CHUNK * GROUP
+    step = chunk_rows(rows)
+    size = step * GROUP
 
     def lay(values):
         return jnp.concatenate(
             [
-                jnp.concatenate([v[k * GROUP : (k + 1) * GROUP] for k in range(CHUNK)], axis=1)
+                jnp.concatenate([v[k * GROUP : (k + 1) * GROUP] for k in range(step)], axis=1)
                 for v in values
             ],
             axis=0,
@@ -125,7 +130,7 @@
         at = pl.ds(pl.multiple_of(chunk * size, size), size)
         base = mixed_ref[at, :]
         weight = weight_ref[at, :]
-        y = chunk * CHUNK + iota((size, 1), 0) // GROUP
+        y = chunk * step + iota((size, 1), 0) // GROUP
         eta = 2.0 * y.astype(F32) / rows - 1.0
         feats = (base, base * xi, base * eta)
         right = jnp.concatenate(split(lay(feats)), axis=0)
@@ -133,7 +138,7 @@
         return acc + lax.dot_general(left, right, NT, preferred_element_type=F32)
 
     side = 3 * GROUP
-    sums = lax.fori_loop(0, rows // CHUNK, body, jnp.zeros((2 * side, 2 * side), F32), unroll=UNROLL)
+    sums = lax.fori_loop(0, rows // step, body, jnp.zeros((2 * side, 2 * side), F32))
     return sums[:side, :side] + (sums[:side, side:] + sums[side:, :side] + sums[side:, side:])
 
 
@@ -223,9 +228,6 @@
     flipped = jnp.transpose(slots[epoch])
     pack[0] = flipped[:EDGE]
     pack[1] = flipped[cols - EDGE :]
-    for load in loads[1:4]:
-        load.wait()
-    make_weight(srow_ref, scol_ref, cov_ref, weight_ref)
     pl.semaphore_wait(barrier, epochs * tiles - 1)
 
     def block_copy(e, source):
@@ -251,8 +253,9 @@
         def _():
             edge_copy(e, 1, epoch).start()
 
-    for load in loads[4:]:
+    for load in loads[1:]:
         load.wait()
+    make_weight(srow_ref, scol_ref, cov_ref, weight_ref)
     make_bands(rowp_ref, colp_ref, profile_ref, row_band_ref, col_band_ref, top - taps // 2)
     fill_rest(mixed_ref, science_ref[0], count)
     high = across_ref.shape[1]

time: 31.9 us -> 28.7 us (0.90)
  Pallas kernels: 30.1 us -> 26.9 us
    pallas_call x1, Pallas kernels: 30.1 us -> 26.9 us  [local(): pl.pallas_call(functools.partial(kernel, cols * tiles, top), out_shape=ja...]
where the time goes in v3:
time: 28.7 us; the launch traced here: 28.5 us
  Pallas kernels  26.9 us (94%)
  local copies, waits for them, and re-layouts  1.62 us (6%)
    pallas_call x1, Pallas kernels, local(): pl.pallas_call(functools.partial(kernel, cols * tiles, top), out_shape=ja...  26.9 us
    unnamed x1, local copies, waits for them, and re-layouts  1.62 us

profile of v3, /device:TPU:0, one launch (start us, length us, event | category | flops | bytes accessed | tf_op | source)
XLA Modules:
  0.0 28.5 jit_solution(203454201642357142)
XLA Ops:
  0.0 26.9 %shard_map.73 = f32[1,384,128]{2,1,0:T(8,128)} custom-call(f32[96,128]{1,0:T(8,128)} %template_in.1, f32[1,384,128]{2,1,0:T(8,128)} %science_in.1, f32[12,21]{1,0:T(8,128)} %rowp_in.1, f32[12,21]{1,0:T(8,128)} %colp_in.1, s32[1,64]{1,0:T(1,128)} %cov_in.1, s32[1,64]{1,0:T(1,128)} %bitcast.2, s32[1,64]{1,0:T(1,128)} %bitcast.3), custom_call_target="tpu_custom_call" | custom-call | tf_op jit(solution)/shard_map/pallas_call | solution.py:348
  26.9 1.6 %copy.9 = f32[1,384,128]{2,1,0:T(8,128)} copy(f32[1,384,128]{2,1,0:T(8,128)} %shard_map.73) | data formatting | bytes 393216

commit v4 on v3

--- a/solution.py
+++ b/solution.py
@@ -155,9 +155,9 @@
     unknowns = [k for k in range(side) if (k % GROUP < count) or k == count]
     for p in unknowns:
         pivot_row = system[p : p + 1, :]
-        factor = system[:, p : p + 1] / system[p : p + 1, p : p + 1]
-        factor = jnp.where(row[:, :1] == p, 0.0, factor)
-        system = system - factor * pivot_row
+        scaled = pivot_row / system[p : p + 1, p : p + 1]
+        factor = jnp.where(row[:, :1] == p, 0.0, system[:, p : p + 1])
+        system = system - factor * scaled
     diagonal = jnp.sum(jnp.where(row == col, system, 0.0), axis=1, keepdims=True)
     return system[:, side : side + 1] / diagonal
 

time: 28.7 us -> 28.5 us (level)
  no operation moved by 1% of the time
where the time goes in v4:
time: 28.5 us; the launch traced here: 28.4 us
  Pallas kernels  26.7 us (94%)
  local copies, waits for them, and re-layouts  1.62 us (6%)
    pallas_call x1, Pallas kernels, local(): pl.pallas_call(functools.partial(kernel, cols * tiles, top), out_shape=ja...  26.7 us
    unnamed x1, local copies, waits for them, and re-layouts  1.62 us

profile of v4, /device:TPU:0, one launch (start us, length us, event | category | flops | bytes accessed | tf_op | source)
XLA Modules:
  0.0 28.4 jit_solution(4581177154298112802)
XLA Ops:
  0.0 26.7 %shard_map.73 = f32[1,384,128]{2,1,0:T(8,128)} custom-call(f32[96,128]{1,0:T(8,128)} %template_in.1, f32[1,384,128]{2,1,0:T(8,128)} %science_in.1, f32[12,21]{1,0:T(8,128)} %rowp_in.1, f32[12,21]{1,0:T(8,128)} %colp_in.1, s32[1,64]{1,0:T(1,128)} %cov_in.1, s32[1,64]{1,0:T(1,128)} %bitcast.2, s32[1,64]{1,0:T(1,128)} %bitcast.3), custom_call_target="tpu_custom_call" | custom-call | tf_op jit(solution)/shard_map/pallas_call | solution.py:348
  26.7 1.6 %copy.9 = f32[1,384,128]{2,1,0:T(8,128)} copy(f32[1,384,128]{2,1,0:T(8,128)} %shard_map.73) | data formatting | bytes 393216
